TPU v7x, 32 devices: a whole 2x2x4 slice. The times are simulated.
32 devices in a mesh: seq: 4 (over z), dp: 8 (over y, x, core).
Axes of the slice: x: 2, y: 2, z: 4, core: 2. Of those that a mesh axis runs over, the one named last changes fastest.
Arguments:
- stream: float32 [8, 512, 1152], P('dp', 'seq'), may hold values from -50 to 50
- stream_grad: float32 [8, 512, 1152], P('dp', 'seq'), may hold values from -6 to 6
- lengths: int32 [8, 4], P('dp'), may hold values from 1 to 384, 512 in all within a row
- w_qkv: bfloat16 [1152, 1536], P(('seq', 'dp')), may hold values from -0.1875 to 0.1875
- w_out: bfloat16 [1024, 1152], P(('seq', 'dp')), may hold values from -0.1875 to 0.1875
- w_gate: bfloat16 [6912, 1152], P(('seq', 'dp')), may hold values from -0.1875 to 0.1875
- w_up: bfloat16 [6912, 1152], P(('seq', 'dp')), may hold values from -0.1875 to 0.1875
- w_down: bfloat16 [6912, 1152], P(('seq', 'dp')), may hold values from -0.078125 to 0.078125
- g_attn_in: float32 [1152], replicated, may hold values from 0.25 to 1.75
- g_query: float32 [256], replicated, may hold values from 0.25 to 1.75
- g_key: float32 [256], replicated, may hold values from 0.25 to 1.75
- g_attn_out: float32 [1152], replicated, may hold values from 0.25 to 1.75
- g_ffn_in: float32 [1152], replicated, may hold values from 0.25 to 1.75
- g_ffn_out: float32 [1152], replicated, may hold values from 0.25 to 1.75
Outputs:
- result: float32 [8, 512, 1152], P('dp', 'seq')
- input_grad: float32 [8, 512, 1152], P('dp', 'seq')
- grad_w_qkv: float32 [1152, 1536], P(('seq', 'dp'))
- grad_w_out: float32 [1024, 1152], P(('seq', 'dp'))
- grad_w_gate: float32 [6912, 1152], P(('seq', 'dp'))
- grad_w_up: float32 [6912, 1152], P(('seq', 'dp'))
- grad_w_down: float32 [6912, 1152], P(('seq', 'dp'))
- grad_g_attn_in: float32 [1152], P(('seq', 'dp'))
- grad_g_query: float32 [256], P(('seq', 'dp'))
- grad_g_key: float32 [256], P(('seq', 'dp'))
- grad_g_attn_out: float32 [1152], P(('seq', 'dp'))
- grad_g_ffn_in: float32 [1152], P(('seq', 'dp'))
- grad_g_ffn_out: float32 [1152], P(('seq', 'dp'))
Inputs may be any that keep to these rules, and one draw needn't show every extreme that they name: Each row lists the lengths of the 4 sequences packed in order into one group; they sum to 512.
All inputs are finite; a program needn't handle non-finite values.
Results may differ from a plain program's by a relative error of at most 0.015.
Values may be sent and summed in bfloat16 or wider, within the bound.
A program may use at most 128 MiB of HBM per device.

v0:
```python
import math
import jax
import jax.numpy as jnp
from jax import lax
from jax.sharding import PartitionSpec as P

HEADS = 4
HEAD_DIM = 256
WINDOW = 512
EPSILON = 1e-06
GELU_SLOPE = math.sqrt(2.0 / math.pi)
GELU_CUBIC = 0.044715


def passed_along(value, axis, by):
    length = lax.axis_size(axis)
    pairs = [(i, i + by) for i in range(length) if 0 <= i + by < length]
    return lax.ppermute(value, axis, pairs)


def inv_root(vector):
    return lax.rsqrt(jnp.mean(vector * vector, axis=-1, keepdims=True) + EPSILON)


def norm_back(grad, unit_part, root_part, gain):
    scaled = grad * gain
    return root_part * (scaled - unit_part * jnp.mean(scaled * unit_part, axis=-1, keepdims=True))


def gelu_pair(gate):
    inner = jnp.tanh(GELU_SLOPE * (gate + GELU_CUBIC * gate * gate * gate))
    gelu_value = 0.5 * gate * (1.0 + inner)
    gelu_slope = 0.5 * (1.0 + inner) + 0.5 * gate * (1.0 - inner * inner) * GELU_SLOPE * (
        1.0 + 3.0 * GELU_CUBIC * gate * gate
    )
    return (gelu_value, gelu_slope)


def turn_half(vector):
    half = vector.shape[-1] // 2
    return jnp.concatenate([-vector[..., half:], vector[..., :half]], axis=-1)


def seq_begin(index, starts):
    return jnp.max(jnp.where(starts[None, :] <= index[:, None], starts[None, :], 0), axis=1)


def rope_tables(position, head):
    freq = jnp.exp(-math.log(10000.0) * jnp.arange(head // 2, dtype=jnp.float32) * (2.0 / head))
    angle = position[:, None] * freq[None, :]
    angle = jnp.concatenate([angle, angle], axis=1)
    return (jnp.cos(angle), jnp.sin(angle))


def dot32(left, right):
    return jnp.dot(left, right, preferred_element_type=jnp.float32)


def contract_rows(left, right):
    return lax.dot_general(
        left, right, (((0,), (0,)), ((), ())), preferred_element_type=jnp.float32
    )


def contract_cols(left, right):
    return lax.dot_general(
        left, right, (((1,), (1,)), ((), ())), preferred_element_type=jnp.float32
    )


def ffn_forward_fold(tokens_b, pieces):
    gate_rows, up_rows, down_rows = pieces
    gate_part = contract_cols(tokens_b, gate_rows)
    up_part = contract_cols(tokens_b, up_rows)
    gelu_value, gelu_slope = gelu_pair(gate_part)
    hidden = (gelu_value * up_part).astype(jnp.bfloat16)
    out_total = dot32(hidden, down_rows)
    return (out_total, gate_part, up_part)


def ffn_backward_fold(grad_b, gate_all, up_all, pieces):
    gate_rows, up_rows, down_rows = pieces
    hidden_grad = contract_cols(grad_b, down_rows)
    gelu_value, gelu_slope = gelu_pair(gate_all)
    dgate_b = (hidden_grad * up_all * gelu_slope).astype(jnp.bfloat16)
    dup_b = (hidden_grad * gelu_value).astype(jnp.bfloat16)
    in_total = dot32(dgate_b, gate_rows) + dot32(dup_b, up_rows)
    return (in_total, dgate_b, dup_b)


def ffn_weight_terms(tokens_b, grad_b, gate_all, up_all, dgate_all, dup_all):
    gelu_value, gelu_slope = gelu_pair(gate_all)
    hidden = (gelu_value * up_all).astype(jnp.bfloat16)
    return jnp.concatenate(
        [
            contract_rows(dgate_all, tokens_b),
            contract_rows(dup_all, tokens_b),
            contract_rows(hidden, grad_b),
        ],
        axis=1,
    )


def local(
    stream,
    stream_grad,
    lengths,
    w_qkv,
    w_out,
    w_gate,
    w_up,
    w_down,
    g_attn_in,
    g_query,
    g_key,
    g_attn_out,
    g_ffn_in,
    g_ffn_out,
):
    rows_in = stream[0]
    rows_grad = stream_grad[0]
    lens = lengths[0]
    rows = rows_in.shape[0]
    width = rows_in.shape[1]
    qwidth = HEADS * HEAD_DIM
    hops = (WINDOW + rows - 2) // rows
    keys = (hops + 1) * rows
    scale = 1.0 / math.sqrt(HEAD_DIM)
    qkv_full, out_full = (
        lax.all_gather(w_qkv, ("seq", "dp"), axis=0, tiled=True),
        lax.all_gather(w_out, ("seq", "dp"), axis=0, tiled=True),
    )
    block_id = lax.axis_index("seq")
    starts = jnp.cumsum(lens) - lens
    own_index = block_id * rows + jnp.arange(rows, dtype=jnp.int32)
    key_index = block_id * rows - hops * rows + jnp.arange(keys, dtype=jnp.int32)
    own_begin = seq_begin(own_index, starts)
    key_begin = seq_begin(key_index, starts)
    mask = (
        (key_index[None, :] >= 0)
        & (key_begin[None, :] == own_begin[:, None])
        & (key_index[None, :] <= own_index[:, None])
        & (own_index[:, None] - key_index[None, :] < WINDOW)
    )
    full_mask = mask[:, None, :]
    cos_t, sin_t = rope_tables((own_index - own_begin).astype(jnp.float32), HEAD_DIM)
    root_attn = inv_root(rows_in)
    unit_attn = rows_in * root_attn
    attn_input = (unit_attn * g_attn_in).astype(jnp.bfloat16)
    projected = dot32(attn_input, qkv_full)
    query = projected[:, :qwidth].reshape(rows, HEADS, HEAD_DIM)
    key_raw = projected[:, qwidth : qwidth + HEAD_DIM]
    value_raw = projected[:, qwidth + HEAD_DIM :]
    root_query = inv_root(query)
    unit_query = query * root_query
    query_norm = unit_query * g_query
    root_key = inv_root(key_raw)
    unit_key = key_raw * root_key
    key_norm = unit_key * g_key
    query_rot = query_norm * cos_t[:, None, :] + turn_half(query_norm) * sin_t[:, None, :]
    key_rot = key_norm * cos_t + turn_half(key_norm) * sin_t
    query_b = query_rot.astype(jnp.bfloat16)
    kv_own = jnp.concatenate([key_rot.astype(jnp.bfloat16), value_raw.astype(jnp.bfloat16)], axis=1)
    earlier = []
    for hop in range(hops, 0, -1):
        earlier.append(passed_along(kv_own, "seq", hop))
    kv_all = jnp.concatenate(earlier + [kv_own], axis=0)
    keys_b = kv_all[:, :HEAD_DIM]
    values_b = kv_all[:, HEAD_DIM:]
    scores = jnp.einsum("rhd,kd->rhk", query_b, keys_b, preferred_element_type=jnp.float32) * scale
    logsum = jnp.log(jnp.sum(jnp.where(full_mask, jnp.exp(scores), 0.0), axis=-1))
    probs = jnp.where(full_mask, jnp.exp(scores - logsum[..., None]), 0.0)
    probs_b = probs.astype(jnp.bfloat16)
    mixed = jnp.einsum("rhk,kd->rhd", probs_b, values_b, preferred_element_type=jnp.float32)
    mixed_b = mixed.reshape(rows, qwidth).astype(jnp.bfloat16)
    attn_out = dot32(mixed_b, out_full)
    root_post = inv_root(attn_out)
    unit_post = attn_out * root_post
    hidden_in = rows_in + unit_post * g_attn_out
    root_ffn = inv_root(hidden_in)
    unit_ffn = hidden_in * root_ffn
    ffn_input = (unit_ffn * g_ffn_in).astype(jnp.bfloat16)
    tokens_b = lax.all_gather(ffn_input, "seq", axis=0, tiled=True)
    out_part, gate_all, up_all = ffn_forward_fold(
        tokens_b,
        (
            lax.all_gather(w_gate, "dp", axis=0, tiled=True),
            lax.all_gather(w_up, "dp", axis=0, tiled=True),
            lax.all_gather(w_down, "dp", axis=0, tiled=True),
        ),
    )
    ffn_out = lax.psum_scatter(out_part, "seq", scatter_dimension=0, tiled=True)
    root_out = inv_root(ffn_out)
    unit_out = ffn_out * root_out
    result = hidden_in + unit_out * g_ffn_out
    grad_g_ffn_out = jnp.sum(rows_grad * unit_out, axis=0)
    ffn_grad_b = norm_back(rows_grad, unit_out, root_out, g_ffn_out).astype(jnp.bfloat16)
    grads_b = lax.all_gather(ffn_grad_b, "seq", axis=0, tiled=True)
    in_part, dgate_all, dup_all = ffn_backward_fold(
        grads_b,
        gate_all,
        up_all,
        (
            lax.all_gather(w_gate, "dp", axis=0, tiled=True),
            lax.all_gather(w_up, "dp", axis=0, tiled=True),
            lax.all_gather(w_down, "dp", axis=0, tiled=True),
        ),
    )
    ffn_in_grad = lax.psum_scatter(in_part, "seq", scatter_dimension=0, tiled=True)
    ffn_terms = lax.psum_scatter(
        ffn_weight_terms(tokens_b, grads_b, gate_all, up_all, dgate_all, dup_all).astype(
            jnp.bfloat16
        ),
        "dp",
        scatter_dimension=0,
        tiled=True,
    ).astype(jnp.float32)
    grad_w_gate = ffn_terms[:, :width]
    grad_w_up = ffn_terms[:, width : 2 * width]
    grad_w_down = ffn_terms[:, 2 * width :]
    grad_g_ffn_in = jnp.sum(ffn_in_grad * unit_ffn, axis=0)
    hidden_grad_in = rows_grad + norm_back(ffn_in_grad, unit_ffn, root_ffn, g_ffn_in)
    grad_g_attn_out = jnp.sum(hidden_grad_in * unit_post, axis=0)
    attn_grad_b = norm_back(hidden_grad_in, unit_post, root_post, g_attn_out).astype(jnp.bfloat16)
    mixed_grad_b = contract_cols(attn_grad_b, out_full).astype(jnp.bfloat16)
    mixed_grad3 = mixed_grad_b.reshape(rows, HEADS, HEAD_DIM)
    delta = jnp.sum(
        mixed_grad3.astype(jnp.float32)
        * mixed_b.reshape(rows, HEADS, HEAD_DIM).astype(jnp.float32),
        axis=-1,
    )
    scores_again = (
        jnp.einsum("rhd,kd->rhk", query_b, keys_b, preferred_element_type=jnp.float32) * scale
    )
    probs_again = jnp.where(full_mask, jnp.exp(scores_again - logsum[..., None]), 0.0)
    probs_again_b = probs_again.astype(jnp.bfloat16)
    value_grad_all = jnp.einsum(
        "rhk,rhd->kd", probs_again_b, mixed_grad3, preferred_element_type=jnp.float32
    )
    prob_grad = jnp.einsum("rhd,kd->rhk", mixed_grad3, values_b, preferred_element_type=jnp.float32)
    score_grad_b = (probs_again * (prob_grad - delta[..., None])).astype(jnp.bfloat16)
    query_rot_grad = (
        jnp.einsum("rhk,kd->rhd", score_grad_b, keys_b, preferred_element_type=jnp.float32) * scale
    )
    key_grad_all = (
        jnp.einsum("rhk,rhd->kd", score_grad_b, query_b, preferred_element_type=jnp.float32) * scale
    )
    kv_grad_all = jnp.concatenate([key_grad_all, value_grad_all], axis=1)
    kv_grad = kv_grad_all[hops * rows :]
    for hop in range(1, hops + 1):
        block = kv_grad_all[(hops - hop) * rows : (hops - hop + 1) * rows]
        kv_grad = kv_grad + passed_along(block.astype(jnp.bfloat16), "seq", -hop).astype(
            block.dtype
        )
    key_rot_grad = kv_grad[:, :HEAD_DIM]
    value_grad = kv_grad[:, HEAD_DIM:]
    query_norm_grad = query_rot_grad * cos_t[:, None, :] - turn_half(
        query_rot_grad * sin_t[:, None, :]
    )
    key_norm_grad = key_rot_grad * cos_t - turn_half(key_rot_grad * sin_t)
    grad_g_query = jnp.sum(query_norm_grad * unit_query, axis=(0, 1))
    grad_g_key = jnp.sum(key_norm_grad * unit_key, axis=0)
    query_grad = norm_back(query_norm_grad, unit_query, root_query, g_query)
    key_grad = norm_back(key_norm_grad, unit_key, root_key, g_key)
    qkv_grad_b = jnp.concatenate(
        [query_grad.reshape(rows, qwidth), key_grad, value_grad], axis=1
    ).astype(jnp.bfloat16)
    attn_in_grad = contract_cols(qkv_grad_b, qkv_full)
    grad_g_attn_in = jnp.sum(attn_in_grad * unit_attn, axis=0)
    input_grad = hidden_grad_in + norm_back(attn_in_grad, unit_attn, root_attn, g_attn_in)
    gain_terms = jnp.stack([grad_g_attn_in, grad_g_attn_out, grad_g_ffn_in, grad_g_ffn_out])
    head_terms = jnp.stack([grad_g_query, grad_g_key])
    out_term = contract_rows(mixed_b, attn_grad_b)
    qkv_term = contract_rows(attn_input, qkv_grad_b)
    owned_qkv, owned_out, owned_gains, owned_heads = (
        lax.psum_scatter(qkv_term, ("seq", "dp"), scatter_dimension=0, tiled=True),
        lax.psum_scatter(out_term, ("seq", "dp"), scatter_dimension=0, tiled=True),
        lax.psum_scatter(gain_terms, ("seq", "dp"), scatter_dimension=1, tiled=True),
        lax.psum_scatter(head_terms, ("seq", "dp"), scatter_dimension=1, tiled=True),
    )
    return (
        result[None],
        input_grad[None],
        owned_qkv,
        owned_out,
        grad_w_gate,
        grad_w_up,
        grad_w_down,
        owned_gains[0],
        owned_heads[0],
        owned_heads[1],
        owned_gains[1],
        owned_gains[2],
        owned_gains[3],
    )


def solution(mesh):
    return jax.shard_map(
        local,
        mesh=mesh,
        in_specs=(
            P("dp", "seq", None),
            P("dp", "seq", None),
            P("dp", None),
            P(("seq", "dp"), None),
            P(("seq", "dp"), None),
            P(("seq", "dp"), None),
            P(("seq", "dp"), None),
            P(("seq", "dp"), None),
            P(),
            P(),
            P(),
            P(),
            P(),
            P(),
        ),
        out_specs=(
            P("dp", "seq", None),
            P("dp", "seq", None),
            P(("seq", "dp"), None),
            P(("seq", "dp"), None),
            P(("seq", "dp"), None),
            P(("seq", "dp"), None),
            P(("seq", "dp"), None),
            P(("seq", "dp")),
            P(("seq", "dp")),
            P(("seq", "dp")),
            P(("seq", "dp")),
            P(("seq", "dp")),
            P(("seq", "dp")),
        ),
        check_vma=False,
    )
```

profile of v0, /device:TPU:0, one launch (start us, length us, event | category | flops | bytes accessed | tf_op | source)
XLA Modules:
  0.0 682.3 jit_solution(9453058917675593302)
XLA Ops:
  13.7 60.8 %all-gather.21.cloned.1.call-done = bf16[32,36,1536]{2,1,0:T(8,128)(2,1)} async-done(((bf16[1,36,1536]{2,1,0:T(8,128)(2,1)}), bf16[32,36,1536]{2,1,0:T(8,128)(2,1)}) %all-gather.21.cloned.1.call-update) | async-done | bytes 3538960 | tf_op jit(solution)/shard_map/all_gather | solution.py:130
  85.0 4.7 collective-permute-start.1
  113.6 23.7 %all-gather.9.cloned.1.call-done = bf16[1024,1152]{1,0:T(8,128)(2,1)} async-done(((bf16[32,1152]{1,0:T(8,128)(2,1)}), bf16[1024,1152]{1,0:T(8,128)(2,1)}) %all-gather.9.cloned.1.call-update) | async-done | bytes 2359312 | tf_op jit(solution)/shard_map/all_gather | solution.py:131
  143.9 29.8 %all-gather.13.cloned.1.call-done = bf16[1728,1152]{1,0:T(8,128)(2,1)} async-done(((bf16[216,1152]{1,0:T(8,128)(2,1)}), bf16[1728,1152]{1,0:T(8,128)(2,1)}) %all-gather.13.cloned.1.call-update) | async-done | bytes 3981328 | tf_op jit(solution)/shard_map/all_gather | solution.py:187
  173.7 32.3 %all-gather.11.cloned.1.call-done = bf16[512,1152]{1,0:T(8,128)(2,1)} async-done(((bf16[128,1152]{1,0:T(8,128)(2,1)}), bf16[512,1152]{1,0:T(8,128)(2,1)}) %all-gather.11.cloned.1.call-update) | async-done | bytes 1179664 | tf_op jit(solution)/shard_map/all_gather | solution.py:183
  206.0 6.8 fusion.51
  212.8 29.9 %all-gather.15.cloned.1.call-done = bf16[1728,1152]{1,0:T(8,128)(2,1)} async-done(((bf16[216,1152]{1,0:T(8,128)(2,1)}), bf16[1728,1152]{1,0:T(8,128)(2,1)}) %all-gather.15.cloned.1.call-update) | async-done | bytes 3981328 | tf_op jit(solution)/shard_map/all_gather | solution.py:188
  242.7 9.3 %multiply_convert_fusion.1 = (bf16[512,1728]{0,1:T(8,128)(2,1)}, f32[512,1728]{0,1:T(8,128)}) fusion(f32[512,1728]{0,1:T(8,128)} %fusion.51, bf16[512,1152]{1,0:T(8,128)(2,1)} %all-gather.11.cloned.1.call-done, bf16[1728,1152]{1,0:T(8,128)(2,1)} %all-gather.15.cloned.1.call-done), kind=kOutput, calls=%fused_computation.15 | convolution fusion | flops 2047279104 | bytes 14008320 | tf_op jit(solution)/shard_map/dot_general | solution.py:66
  252.0 28.2 %all-gather.17.cloned.1.call-done = bf16[1728,1152]{1,0:T(8,128)(2,1)} async-done(((bf16[216,1152]{1,0:T(8,128)(2,1)}), bf16[1728,1152]{1,0:T(8,128)(2,1)}) %all-gather.17.cloned.1.call-update) | async-done | bytes 3981328 | tf_op jit(solution)/shard_map/all_gather | solution.py:189
  280.2 6.7 fusion.52
  286.9 47.8 %reduce-scatter.11.cloned.1.call-done = f32[128,1152]{1,0:T(8,128)} async-done(((f32[512,1152]{1,0:T(8,128)}), f32[128,1152]{1,0:T(8,128)}) %reduce-scatter.11.cloned.1.call-update) | async-done | bytes 589840 | tf_op jit(solution)/shard_map/reduce_scatter | solution.py:192
  341.2 29.2 %all-gather.19.cloned.1.call-done = bf16[512,1152]{1,0:T(8,128)(2,1)} async-done(((bf16[128,1152]{1,0:T(8,128)(2,1)}), bf16[512,1152]{1,0:T(8,128)(2,1)}) %all-gather.19.cloned.1.call-update) | async-done | bytes 1179664 | tf_op jit(solution)/shard_map/all_gather | solution.py:198
  370.4 9.5 %multiply_convert_fusion = (bf16[512,1728]{0,1:T(8,128)(2,1)S(1)}, bf16[512,1728]{0,1:T(8,128)(2,1)S(1)}) fusion(f32[512,1728]{0,1:T(8,128)} %fusion.51, f32[512,1728]{0,1:T(8,128)} %get-tuple-element.66, bf16[512,1152]{1,0:T(8,128)(2,1)} %all-gather.19.cloned.1.call-done, bf16[1728,1152]{1,0:T(8,128)(2,1)} %all-gather.17.cloned.1.call-done), kind=kOutput, calls=%fused_computation.14 | convolution fusion | flops 2058780672 | bytes 15777792 | tf_op jit(solution)/shard_map/dot_general | solution.py:66
  383.3 4.1 convolution_add_fusion
  387.7 4.4 convolution_convert_fusion
  397.0 5.0 pad_maximum_fusion
  406.2 28.3 %reduce-scatter.13.cloned.1.call-done = f32[128,1152]{1,0:T(8,128)} async-done(((f32[512,1152]{1,0:T(8,128)}), f32[128,1152]{1,0:T(8,128)}) %reduce-scatter.13.cloned.1.call-update) | async-done | bytes 589840 | tf_op jit(solution)/shard_map/reduce_scatter | solution.py:209
  468.7 4.8 collective-permute-done.5
  489.9 5.3 fusion.34
  495.2 103.8 %fusion = f32[40,1536]{1,0:T(8,128)} fusion(f32[1152,1536]{1,0:T(8,128)} %fusion.34), kind=kCustom, calls=%all-reduce-scatter | all-reduce-scatter fusion | flops 1966081 | bytes 7323648
  603.6 7.6 %collective-permute-start.9 = (f32[40,1536]{1,0:T(8,128)}, f32[40,1536]{1,0:T(8,128)}, u32[]{:S(2)}, u32[]{:S(2)}) collective-permute-start(f32[40,1536]{1,0:T(8,128)} %fusion), channel_id=1, source_target_pairs={{0,2},{1,3},{2,4},{3,5},{4,6},{5,7},{6,8},{7,9},{8,10},{9,11},{10,... | collective-permute-start | bytes 737288
  619.9 39.2 %all-reduce.5 = (f32[4,1152]{1,0:T(4,128)S(1)}, f32[2,256]{1,0:T(2,128)S(1)}) all-reduce(f32[4,1152]{1,0:T(4,128)S(1)} %pad_maximum_fusion.7, f32[2,256]{1,0:T(2,128)S(1)} %pad_maximum_fusion.8), channel_id=7, replica_groups=mesh['seq'=4,'dp'=8] {'seq','dp'}, use_global_device_ids=true, to_apply=%region_26.27.clone | all-reduce | flops 5120 | bytes 40960
  662.8 4.1 concatenate.50
  670.7 4.9 reduce-scatter.15.cloned.1.call-done
  (257 shorter events, 137.3 us)
Async XLA Ops:
  7.2 67.3 %all-gather.21.cloned.1.call-start = ((), (), s32[]{:S(2)}) async-start(), calls=%async_computation.13 | async-start | bytes 4055040 | tf_op jit(solution)/shard_map/all_gather | solution.py:130
  7.9 129.4 %all-gather.9.cloned.1.call-start = ((), (), s32[]{:S(2)}) async-start(), calls=%async_computation.4 | async-start | bytes 2433024 | tf_op jit(solution)/shard_map/all_gather | solution.py:131
  8.7 165.1 %all-gather.13.cloned.1.call-start = ((), (), s32[]{:S(2)}) async-start(), calls=%async_computation.6 | async-start | bytes 4478976 | tf_op jit(solution)/shard_map/all_gather | solution.py:187
  9.4 196.6 %all-gather.11.cloned.1.call-start = ((), (), s32[]{:S(2)}) async-start(), calls=%async_computation.5 | async-start | bytes 1474560 | tf_op jit(solution)/shard_map/all_gather | solution.py:183
  83.7 18.7 %collective-permute-start = (bf16[128,512]{1,0:T(8,128)(2,1)}, bf16[128,512]{1,0:T(8,128)(2,1)}, u32[]{:S(2)}, u32[]{:S(2)}) collective-permute-start(bf16[128,512]{1,0:T(8,128)(2,1)} %pad_maximum_fusion.6), channel_id=1, source_target_pairs={} | collective-permute-start | bytes 393224 | tf_op jit(solution)/shard_map/ppermute | solution.py:18
  85.0 18.4 %collective-permute-start.1 = (bf16[128,512]{1,0:T(8,128)(2,1)}, bf16[128,512]{1,0:T(8,128)(2,1)}, u32[]{:S(2)}, u32[]{:S(2)}) collective-permute-start(bf16[128,512]{1,0:T(8,128)(2,1)} %pad_maximum_fusion.6), channel_id=1, source_target_pairs={{0,24},{1,25},{2,26},{3,27},{4,28},{5,29},{6,30},{7,31}} | collective-permute-start | bytes 393224 | tf_op jit(solution)/shard_map/ppermute | solution.py:18
  89.7 14.6 %collective-permute-start.2 = (bf16[128,512]{1,0:T(8,128)(2,1)}, bf16[128,512]{1,0:T(8,128)(2,1)}, u32[]{:S(2)}, u32[]{:S(2)}) collective-permute-start(bf16[128,512]{1,0:T(8,128)(2,1)} %pad_maximum_fusion.6), channel_id=1, source_target_pairs={{0,16},{8,24},{1,17},{9,25},{2,18},{10,26},{3,19},{11,27},{4,20},{... | collective-permute-start | bytes 393224 | tf_op jit(solution)/shard_map/ppermute | solution.py:18
  91.7 13.6 %collective-permute-start.3 = (bf16[128,512]{1,0:T(8,128)(2,1)}, bf16[128,512]{1,0:T(8,128)(2,1)}, u32[]{:S(2)}, u32[]{:S(2)}) collective-permute-start(bf16[128,512]{1,0:T(8,128)(2,1)} %pad_maximum_fusion.6), channel_id=1, source_target_pairs={{0,8},{8,16},{16,24},{1,9},{9,17},{17,25},{2,10},{10,18},{18,26},{... | collective-permute-start | bytes 393224 | tf_op jit(solution)/shard_map/ppermute | solution.py:18
  142.4 100.3 %all-gather.15.cloned.1.call-start = ((), (), s32[]{:S(2)}) async-start(), calls=%async_computation.7 | async-start | bytes 4478976 | tf_op jit(solution)/shard_map/all_gather | solution.py:188
  143.0 137.1 %all-gather.17.cloned.1.call-start = ((), (), s32[]{:S(2)}) async-start(), calls=%async_computation.8 | async-start | bytes 4478976 | tf_op jit(solution)/shard_map/all_gather | solution.py:189
  143.6 191.1 %reduce-scatter.11.cloned.1.call-start = ((), (), s32[]{:S(2)}) async-start(), calls=%async_computation.9 | async-start | bytes 2949120 | tf_op jit(solution)/shard_map/reduce_scatter | solution.py:192
  286.9 83.5 %all-gather.19.cloned.1.call-start = ((), (), s32[]{:S(2)}) async-start(), calls=%async_computation.10 | async-start | bytes 1474560 | tf_op jit(solution)/shard_map/all_gather | solution.py:198
  340.6 93.9 %reduce-scatter.13.cloned.1.call-start = ((), (), s32[]{:S(2)}) async-start(), calls=%async_computation.11 | async-start | bytes 2949120 | tf_op jit(solution)/shard_map/reduce_scatter | solution.py:209
  387.4 280.2 %reduce-scatter.17.cloned.1.call-start = ((), (), s32[]{:S(2)}) async-start(), calls=%async_computation.14 | async-start | bytes 13436928
  402.0 273.5 %reduce-scatter.15.cloned.1.call-start = ((), (), s32[]{:S(2)}) async-start(), calls=%async_computation.12 | async-start | bytes 4866048 | tf_op jit(solution)/shard_map/reduce_scatter | solution.py:277
  457.2 10.5 %collective-permute-start.7 = (bf16[128,512]{1,0:T(8,128)(2,1)}, bf16[128,512]{1,0:T(8,128)(2,1)}, u32[]{:S(2)}, u32[]{:S(2)}) collective-permute-start(bf16[128,512]{1,0:T(8,128)(2,1)} %get-tuple-element.38), channel_id=1, source_target_pairs={} | collective-permute-start | bytes 393224 | tf_op jit(solution)/shard_map/ppermute | solution.py:18
  458.5 10.2 %collective-permute-start.6 = (bf16[128,512]{1,0:T(8,128)(2,1)}, bf16[128,512]{1,0:T(8,128)(2,1)}, u32[]{:S(2)}, u32[]{:S(2)}) collective-permute-start(bf16[128,512]{1,0:T(8,128)(2,1)} %get-tuple-element.39), channel_id=1, source_target_pairs={{24,0},{25,1},{26,2},{27,3},{28,4},{29,5},{30,6},{31,7}} | collective-permute-start | bytes 393224 | tf_op jit(solution)/shard_map/ppermute | solution.py:18
  459.8 13.7 %collective-permute-start.5 = (bf16[128,512]{1,0:T(8,128)(2,1)}, bf16[128,512]{1,0:T(8,128)(2,1)}, u32[]{:S(2)}, u32[]{:S(2)}) collective-permute-start(bf16[128,512]{1,0:T(8,128)(2,1)} %get-tuple-element.40), channel_id=1, source_target_pairs={{16,0},{24,8},{17,1},{25,9},{18,2},{26,10},{19,3},{27,11},{20,4},{... | collective-permute-start | bytes 393224 | tf_op jit(solution)/shard_map/ppermute | solution.py:18
  461.1 12.3 %collective-permute-start.4 = (bf16[128,512]{1,0:T(8,128)(2,1)}, bf16[128,512]{1,0:T(8,128)(2,1)}, u32[]{:S(2)}, u32[]{:S(2)}) collective-permute-start(bf16[128,512]{1,0:T(8,128)(2,1)} %get-tuple-element.37), channel_id=1, source_target_pairs={{8,0},{16,8},{24,16},{9,1},{17,9},{25,17},{10,2},{18,10},{26,18},{... | collective-permute-start | bytes 393224 | tf_op jit(solution)/shard_map/ppermute | solution.py:18
  495.2 121.3 %copy-start.45 = (f32[128]{0:T(128)S(1)}, f32[128]{0:T(128)}, u32[]{:S(2)}) copy-start(f32[128]{0:T(128)} %copy-done.44) | copy-start | bytes 1540
  600.5 62.3 %collective-permute-start.10 = (f32[40,1536]{1,0:T(8,128)}, f32[40,1536]{1,0:T(8,128)}, u32[]{:S(2)}, u32[]{:S(2)}) collective-permute-start(f32[40,1536]{1,0:T(8,128)} %fusion), channel_id=1, source_target_pairs={{0,3},{1,4},{2,5},{3,6},{4,7},{5,8},{6,9},{7,10},{8,11},{9,12},{10... | collective-permute-start | bytes 737288
  603.6 59.2 %collective-permute-start.9 = (f32[40,1536]{1,0:T(8,128)}, f32[40,1536]{1,0:T(8,128)}, u32[]{:S(2)}, u32[]{:S(2)}) collective-permute-start(f32[40,1536]{1,0:T(8,128)} %fusion), channel_id=1, source_target_pairs={{0,2},{1,3},{2,4},{3,5},{4,6},{5,7},{6,8},{7,9},{8,10},{9,11},{10,... | collective-permute-start | bytes 737288
  611.2 51.6 %collective-permute-start.8 = (f32[40,1536]{1,0:T(8,128)}, f32[40,1536]{1,0:T(8,128)}, u32[]{:S(2)}, u32[]{:S(2)}) collective-permute-start(f32[40,1536]{1,0:T(8,128)} %fusion), channel_id=1, source_target_pairs={{0,1},{1,2},{2,3},{3,4},{4,5},{5,6},{6,7},{7,8},{8,9},{9,10},{10,1... | collective-permute-start | bytes 737288
  614.2 48.6 %collective-permute-start.11 = (f32[4,1536]{1,0:T(4,128)}, f32[4,1536]{1,0:T(4,128)}, u32[]{:S(2)}, u32[]{:S(2)}) collective-permute-start(f32[4,1536]{1,0:T(4,128)} %slice.146), channel_id=1, source_target_pairs={{0,4},{1,5},{2,6},{3,7},{4,8},{5,9},{6,10},{7,11},{8,12},{9,13},{1... | collective-permute-start | bytes 73736
  (57 other events, 501.1 us)
Sparse Core Ops, SparseCore 0:
  10.9 63.5 all-gather.20
  77.4 59.8 all-gather.8
  139.2 34.4 all-gather.12
  175.7 30.2 all-gather.10
  207.8 34.9 all-gather.14
  244.5 35.6 all-gather.16
  287.0 47.6 reduce-scatter.10
  340.7 29.6 all-gather.18
  387.5 46.9 reduce-scatter.12
  437.9 104.7 reduce-scatter.16
  548.7 126.7 reduce-scatter.14
where the time goes:
time: 689 us; the launch traced here: 682 us
  waiting for transfers between devices  324 us (47%)
  blocking collectives  143 us (21%)
  matrix products  77.7 us (11%)
  other arithmetic  46.2 us (7%)
  local copies, waits for them, and re-layouts  43.2 us (6%)
  starting transfers between devices  33.3 us (5%)
  between operations  15 us (2%)
    unnamed x2, blocking collectives  143 us
    all_gather x1, waiting for transfers between devices, local(): lax.all_gather(w_qkv, ('seq', 'dp'), axis=0, tiled=True)  60.8 us
    reduce_scatter x1, waiting for transfers between devices, local(): ffn_out = lax.psum_scatter(out_part, 'seq', scatter_dimension=0, tiled=True)  47.8 us
    all_gather x1, waiting for transfers between devices, local(): tokens_b = lax.all_gather(ffn_input, 'seq', axis=0, tiled=True)  32.3 us
    dot_general x5, matrix products, contract_cols(): lax.dot_general(left, right, (((1,), (1,)), ((), ())), preferred_element_...  30.4 us
    all_gather x1, waiting for transfers between devices, local(): lax.all_gather(w_up, 'dp', axis=0, tiled=True)  29.9 us
    all_gather x1, waiting for transfers between devices, local(): lax.all_gather(w_gate, 'dp', axis=0, tiled=True)  29.8 us
    all_gather x1, waiting for transfers between devices, local(): grads_b = lax.all_gather(ffn_grad_b, 'seq', axis=0, tiled=True)  29.2 us
  transfers between devices with their start and end apart: 23, of which 12 were waited for; matrix products, arithmetic and copies ran while one was open for 34% of the time, Pallas kernels for 0%

commit v1 on v0

--- a/solution.py
+++ b/solution.py
@@ -10,6 +10,27 @@
 EPSILON = 1e-06
 GELU_SLOPE = math.sqrt(2.0 / math.pi)
 GELU_CUBIC = 0.044715
+
+
+def laid_out(blocks, dim):
+    shape = list(blocks.shape[1:])
+    shape[dim] *= blocks.shape[0]
+    return jnp.moveaxis(blocks, 0, dim).reshape(shape)
+
+
+def doubled(shard, axis):
+    size, index = (lax.axis_size(axis), lax.axis_index(axis))
+    tiles, bit = (shard[None], 1)
+    while bit < size:
+        received = lax.ppermute(tiles, axis, [(i, i ^ bit) for i in range(size)])
+        low = index & bit == 0
+        tiles = jnp.concatenate([jnp.where(low, tiles, received), jnp.where(low, received, tiles)])
+        bit *= 2
+    return tiles
+
+
+def collect(x, axis, dim):
+    return laid_out(doubled(x, axis), dim)
 
 
 def passed_along(value, axis, by):
@@ -127,7 +148,7 @@
     keys = (hops + 1) * rows
     scale = 1.0 / math.sqrt(HEAD_DIM)
     qkv_full, out_full = (
-        lax.all_gather(w_qkv, ("seq", "dp"), axis=0, tiled=True),
+        collect(w_qkv, ("seq", "dp"), 0),
         lax.all_gather(w_out, ("seq", "dp"), axis=0, tiled=True),
     )
     block_id = lax.axis_index("seq")

time: 689 us -> 743 us (1.078)
  waiting for transfers between devices: 324 us -> 355 us
  starting transfers between devices: 33.3 us -> 42.1 us
    ppermute x0 -> x5, waiting for transfers between devices: none -> 115 us  [doubled(): received = lax.ppermute(tiles, axis, [(i, i ^ bit) for i in range(size)])]
    all_gather x1 -> x0, waiting for transfers between devices: 60.8 us -> none  [local(): lax.all_gather(w_qkv, ('seq', 'dp'), axis=0, tiled=True)]
    all_gather x1, waiting for transfers between devices: 23.7 us -> 0.01 us  [local(): lax.all_gather(w_out, ('seq', 'dp'), axis=0, tiled=True)]
    ppermute x0 -> x5, starting transfers between devices: none -> 9.18 us  [doubled(): received = lax.ppermute(tiles, axis, [(i, i ^ bit) for i in range(size)])]
    unnamed x126 -> x129, local copies, waits for them, and re-layouts: 21 us -> 17.2 us
  transfers between devices with their start and end apart: 23 -> 27, of which waited for: 12 -> 15; matrix products, arithmetic and copies ran while one was open for 34% -> 32% of each run, Pallas kernels for 0% -> 0%
where the time goes in v1:
time: 743 us; the launch traced here: 733 us
  waiting for transfers between devices  355 us (48%)
  blocking collectives  144 us (19%)
  matrix products  77.1 us (10%)
  other arithmetic  53 us (7%)
  local copies, waits for them, and re-layouts  45.4 us (6%)
  starting transfers between devices  42.1 us (6%)
  between operations  15.7 us (2%)
    unnamed x2, blocking collectives  144 us
    ppermute x5, waiting for transfers between devices, doubled(): received = lax.ppermute(tiles, axis, [(i, i ^ bit) for i in range(size)])  115 us
    reduce_scatter x1, waiting for transfers between devices, local(): ffn_out = lax.psum_scatter(out_part, 'seq', scatter_dimension=0, tiled=True)  47.8 us
    all_gather x1, waiting for transfers between devices, local(): lax.all_gather(w_gate, 'dp', axis=0, tiled=True)  36.8 us
    all_gather x1, waiting for transfers between devices, local(): lax.all_gather(w_up, 'dp', axis=0, tiled=True)  30.7 us
    dot_general x5, matrix products, contract_cols(): lax.dot_general(left, right, (((1,), (1,)), ((), ())), preferred_element_...  30.4 us
    all_gather x1, waiting for transfers between devices, local(): grads_b = lax.all_gather(ffn_grad_b, 'seq', axis=0, tiled=True)  29.5 us
    reduce_scatter x1, waiting for transfers between devices, local(): lax.psum_scatter(in_part, 'seq', scatter_dimension=0, tiled=True)  28.2 us
  transfers between devices with their start and end apart: 27, of which 15 were waited for; matrix products, arithmetic and copies ran while one was open for 32% of the time, Pallas kernels for 0%

profile of v1, /device:TPU:0, one launch (start us, length us, event | category | flops | bytes accessed | tf_op | source)
XLA Modules:
  0.0 733.0 jit_solution(9301193430338061364)
XLA Ops:
  12.8 6.3 collective-permute-done.1
  21.0 10.9 %collective-permute-done.2 = bf16[4,36,1536]{2,1,0:T(8,128)(2,1)S(1)} collective-permute-done((bf16[4,36,1536]{2,1,0:T(8,128)(2,1)S(1)}, bf16[4,36,1536]{2,1,0:T(8,128)(2,1)S(1)}, u32[]{:S(2)}, u32[]{:S(2)}) %collective-permute-start.2) | collective-permute-done | bytes 442400 | tf_op jit(solution)/shard_map/ppermute | solution.py:25
  34.0 18.8 %collective-permute-done.3 = bf16[8,36,1536]{2,0,1:T(8,128)(2,1)} collective-permute-done((bf16[8,36,1536]{2,0,1:T(8,128)(2,1)S(1)}, bf16[8,36,1536]{2,0,1:T(8,128)(2,1)}, u32[]{:S(2)}, u32[]{:S(2)}) %collective-permute-start.3) | collective-permute-done | bytes 884768 | tf_op jit(solution)/shard_map/ppermute | solution.py:25
  60.9 78.0 %collective-permute-done.4 = bf16[16,36,1536]{2,0,1:T(8,128)(2,1)} collective-permute-done((bf16[16,36,1536]{2,0,1:T(8,128)(2,1)}, bf16[16,36,1536]{2,0,1:T(8,128)(2,1)}, u32[]{:S(2)}, u32[]{:S(2)}) %collective-permute-start.4) | collective-permute-done | bytes 1769504 | tf_op jit(solution)/shard_map/ppermute | solution.py:25
  155.4 5.3 collective-permute-start.6
  191.8 26.5 %all-gather.9.cloned.1.call-done = bf16[512,1152]{1,0:T(8,128)(2,1)} async-done(((bf16[128,1152]{1,0:T(8,128)(2,1)}), bf16[512,1152]{1,0:T(8,128)(2,1)}) %all-gather.9.cloned.1.call-update) | async-done | bytes 1179664 | tf_op jit(solution)/shard_map/all_gather | solution.py:204
  218.3 36.8 %all-gather.11.cloned.1.call-done = bf16[1728,1152]{1,0:T(8,128)(2,1)} async-done(((bf16[216,1152]{1,0:T(8,128)(2,1)}), bf16[1728,1152]{1,0:T(8,128)(2,1)}) %all-gather.11.cloned.1.call-update) | async-done | bytes 3981328 | tf_op jit(solution)/shard_map/all_gather | solution.py:208
  255.2 6.7 fusion.57
  261.9 30.7 %all-gather.13.cloned.1.call-done = bf16[1728,1152]{1,0:T(8,128)(2,1)} async-done(((bf16[216,1152]{1,0:T(8,128)(2,1)}), bf16[1728,1152]{1,0:T(8,128)(2,1)}) %all-gather.13.cloned.1.call-update) | async-done | bytes 3981328 | tf_op jit(solution)/shard_map/all_gather | solution.py:209
  292.6 9.3 %multiply_convert_fusion.1 = (bf16[512,1728]{0,1:T(8,128)(2,1)}, f32[512,1728]{0,1:T(8,128)}) fusion(f32[512,1728]{0,1:T(8,128)} %fusion.57, bf16[512,1152]{1,0:T(8,128)(2,1)} %all-gather.9.cloned.1.call-done, bf16[1728,1152]{1,0:T(8,128)(2,1)} %all-gather.13.cloned.1.call-done), kind=kOutput, calls=%fused_computation.16 | convolution fusion | flops 2047279104 | bytes 14008320 | tf_op jit(solution)/shard_map/dot_general | solution.py:87
  301.9 28.2 %all-gather.15.cloned.1.call-done = bf16[1728,1152]{1,0:T(8,128)(2,1)} async-done(((bf16[216,1152]{1,0:T(8,128)(2,1)}), bf16[1728,1152]{1,0:T(8,128)(2,1)}) %all-gather.15.cloned.1.call-update) | async-done | bytes 3981328 | tf_op jit(solution)/shard_map/all_gather | solution.py:210
  330.1 6.7 fusion.58
  336.9 47.8 %reduce-scatter.11.cloned.1.call-done = f32[128,1152]{1,0:T(8,128)} async-done(((f32[512,1152]{1,0:T(8,128)}), f32[128,1152]{1,0:T(8,128)}) %reduce-scatter.11.cloned.1.call-update) | async-done | bytes 589840 | tf_op jit(solution)/shard_map/reduce_scatter | solution.py:213
  390.8 29.5 %all-gather.17.cloned.1.call-done = bf16[512,1152]{1,0:T(8,128)(2,1)} async-done(((bf16[128,1152]{1,0:T(8,128)(2,1)}), bf16[512,1152]{1,0:T(8,128)(2,1)}) %all-gather.17.cloned.1.call-update) | async-done | bytes 1179664 | tf_op jit(solution)/shard_map/all_gather | solution.py:219
  420.3 9.5 %multiply_convert_fusion = (bf16[512,1728]{0,1:T(8,128)(2,1)S(1)}, bf16[512,1728]{0,1:T(8,128)(2,1)S(1)}) fusion(f32[512,1728]{0,1:T(8,128)} %fusion.57, f32[512,1728]{0,1:T(8,128)} %get-tuple-element.76, bf16[512,1152]{1,0:T(8,128)(2,1)} %all-gather.17.cloned.1.call-done, bf16[1728,1152]{1,0:T(8,128)(2,1)} %all-gather.15.cloned.1.call-done), kind=kOutput, calls=%fused_computation.15 | convolution fusion | flops 2058780672 | bytes 15777792 | tf_op jit(solution)/shard_map/dot_general | solution.py:87
  437.7 4.4 convolution_convert_fusion
  447.1 5.0 pad_maximum_fusion
  456.2 28.2 %reduce-scatter.13.cloned.1.call-done = f32[128,1152]{1,0:T(8,128)} async-done(((f32[512,1152]{1,0:T(8,128)}), f32[128,1152]{1,0:T(8,128)}) %reduce-scatter.13.cloned.1.call-update) | async-done | bytes 589840 | tf_op jit(solution)/shard_map/reduce_scatter | solution.py:230
  518.2 4.6 collective-permute-done.10
  539.3 5.2 fusion.31
  544.5 104.5 %fusion = f32[40,1536]{1,0:T(8,128)} fusion(f32[1152,1536]{1,0:T(8,128)} %fusion.31), kind=kCustom, calls=%all-reduce-scatter | all-reduce-scatter fusion | flops 1966081 | bytes 7323648
  653.7 7.3 collective-permute-start.14
  669.3 39.8 %all-reduce.5 = (f32[4,1152]{1,0:T(4,128)S(1)}, f32[2,256]{1,0:T(2,128)S(1)}) all-reduce(f32[4,1152]{1,0:T(4,128)S(1)} %pad_maximum_fusion.12, f32[2,256]{1,0:T(2,128)S(1)} %pad_maximum_fusion.13), channel_id=7, replica_groups=mesh['seq'=4,'dp'=8] {'seq','dp'}, use_global_device_ids=true, to_apply=%region_26.27.clone | all-reduce | flops 5120 | bytes 40960
  720.6 5.1 reduce-scatter.15.cloned.1.call-done
  (280 shorter events, 162.1 us)
Async XLA Ops:
  7.2 177.4 %all-gather.7.cloned.1.call-start = ((), (), s32[]{:S(2)}) async-start(), calls=%async_computation.4 | async-start | bytes 2433024 | tf_op jit(solution)/shard_map/all_gather | solution.py:152
  19.2 12.8 %collective-permute-start.2 = (bf16[4,36,1536]{2,1,0:T(8,128)(2,1)S(1)}, bf16[4,36,1536]{2,1,0:T(8,128)(2,1)S(1)}, u32[]{:S(2)}, u32[]{:S(2)}) collective-permute-start(bf16[4,36,1536]{2,1,0:T(8,128)(2,1)S(1)} %pad_maximum_fusion.5), channel_id=1, source_target_pairs={{0,4},{1,5},{2,6},{3,7},{4,0},{5,1},{6,2},{7,3},{8,12},{9,13},{10,... | collective-permute-start | bytes 1327112 | tf_op jit(solution)/shard_map/ppermute | solution.py:25
  32.4 20.4 %collective-permute-start.3 = (bf16[8,36,1536]{2,0,1:T(8,128)(2,1)S(1)}, bf16[8,36,1536]{2,0,1:T(8,128)(2,1)}, u32[]{:S(2)}, u32[]{:S(2)}) collective-permute-start(bf16[8,36,1536]{2,0,1:T(8,128)(2,1)S(1)} %copy.114), channel_id=1, source_target_pairs={{0,8},{1,9},{2,10},{3,11},{4,12},{5,13},{6,14},{7,15},{8,0},{9,1},... | collective-permute-start | bytes 2654216 | tf_op jit(solution)/shard_map/ppermute | solution.py:25
  56.6 82.3 %collective-permute-start.4 = (bf16[16,36,1536]{2,0,1:T(8,128)(2,1)}, bf16[16,36,1536]{2,0,1:T(8,128)(2,1)}, u32[]{:S(2)}, u32[]{:S(2)}) collective-permute-start(bf16[16,36,1536]{2,0,1:T(8,128)(2,1)} %copy.117), channel_id=1, source_target_pairs={{0,16},{1,17},{2,18},{3,19},{4,20},{5,21},{6,22},{7,23},{8,24},{9,... | collective-permute-start | bytes 5308424 | tf_op jit(solution)/shard_map/ppermute | solution.py:25
  58.9 159.4 %all-gather.9.cloned.1.call-start = ((), (), s32[]{:S(2)}) async-start(), calls=%async_computation.5 | async-start | bytes 1474560 | tf_op jit(solution)/shard_map/all_gather | solution.py:204
  154.1 19.3 %collective-permute-start.5 = (bf16[128,512]{1,0:T(8,128)(2,1)}, bf16[128,512]{1,0:T(8,128)(2,1)}, u32[]{:S(2)}, u32[]{:S(2)}) collective-permute-start(bf16[128,512]{1,0:T(8,128)(2,1)} %pad_maximum_fusion.11), channel_id=1, source_target_pairs={} | collective-permute-start | bytes 393224 | tf_op jit(solution)/shard_map/ppermute | solution.py:39
  155.4 19.0 %collective-permute-start.6 = (bf16[128,512]{1,0:T(8,128)(2,1)}, bf16[128,512]{1,0:T(8,128)(2,1)}, u32[]{:S(2)}, u32[]{:S(2)}) collective-permute-start(bf16[128,512]{1,0:T(8,128)(2,1)} %pad_maximum_fusion.11), channel_id=1, source_target_pairs={{0,24},{1,25},{2,26},{3,27},{4,28},{5,29},{6,30},{7,31}} | collective-permute-start | bytes 393224 | tf_op jit(solution)/shard_map/ppermute | solution.py:39
  160.7 14.6 %collective-permute-start.7 = (bf16[128,512]{1,0:T(8,128)(2,1)}, bf16[128,512]{1,0:T(8,128)(2,1)}, u32[]{:S(2)}, u32[]{:S(2)}) collective-permute-start(bf16[128,512]{1,0:T(8,128)(2,1)} %pad_maximum_fusion.11), channel_id=1, source_target_pairs={{0,16},{8,24},{1,17},{9,25},{2,18},{10,26},{3,19},{11,27},{4,20},{... | collective-permute-start | bytes 393224 | tf_op jit(solution)/shard_map/ppermute | solution.py:39
  162.7 13.6 %collective-permute-start.8 = (bf16[128,512]{1,0:T(8,128)(2,1)}, bf16[128,512]{1,0:T(8,128)(2,1)}, u32[]{:S(2)}, u32[]{:S(2)}) collective-permute-start(bf16[128,512]{1,0:T(8,128)(2,1)} %pad_maximum_fusion.11), channel_id=1, source_target_pairs={{0,8},{8,16},{16,24},{1,9},{9,17},{17,25},{2,10},{10,18},{18,26},{... | collective-permute-start | bytes 393224 | tf_op jit(solution)/shard_map/ppermute | solution.py:39
  189.7 65.5 %all-gather.11.cloned.1.call-start = ((), (), s32[]{:S(2)}) async-start(), calls=%async_computation.6 | async-start | bytes 4478976 | tf_op jit(solution)/shard_map/all_gather | solution.py:208
  190.4 102.2 %all-gather.13.cloned.1.call-start = ((), (), s32[]{:S(2)}) async-start(), calls=%async_computation.7 | async-start | bytes 4478976 | tf_op jit(solution)/shard_map/all_gather | solution.py:209
  191.0 139.1 %all-gather.15.cloned.1.call-start = ((), (), s32[]{:S(2)}) async-start(), calls=%async_computation.8 | async-start | bytes 4478976 | tf_op jit(solution)/shard_map/all_gather | solution.py:210
  191.6 193.1 %reduce-scatter.11.cloned.1.call-start = ((), (), s32[]{:S(2)}) async-start(), calls=%async_computation.9 | async-start | bytes 2949120 | tf_op jit(solution)/shard_map/reduce_scatter | solution.py:213
  336.8 83.5 %all-gather.17.cloned.1.call-start = ((), (), s32[]{:S(2)}) async-start(), calls=%async_computation.10 | async-start | bytes 1474560 | tf_op jit(solution)/shard_map/all_gather | solution.py:219
  390.5 93.9 %reduce-scatter.13.cloned.1.call-start = ((), (), s32[]{:S(2)}) async-start(), calls=%async_computation.11 | async-start | bytes 2949120 | tf_op jit(solution)/shard_map/reduce_scatter | solution.py:230
  437.4 280.2 %reduce-scatter.17.cloned.1.call-start = ((), (), s32[]{:S(2)}) async-start(), calls=%async_computation.13 | async-start | bytes 13436928
  452.1 273.6 %reduce-scatter.15.cloned.1.call-start = ((), (), s32[]{:S(2)}) async-start(), calls=%async_computation.12 | async-start | bytes 4866048 | tf_op jit(solution)/shard_map/reduce_scatter | solution.py:298
  506.9 10.4 %collective-permute-start.12 = (bf16[128,512]{1,0:T(8,128)(2,1)}, bf16[128,512]{1,0:T(8,128)(2,1)}, u32[]{:S(2)}, u32[]{:S(2)}) collective-permute-start(bf16[128,512]{1,0:T(8,128)(2,1)} %get-tuple-element.44), channel_id=1, source_target_pairs={} | collective-permute-start | bytes 393224 | tf_op jit(solution)/shard_map/ppermute | solution.py:39
  509.4 13.3 %collective-permute-start.10 = (bf16[128,512]{1,0:T(8,128)(2,1)}, bf16[128,512]{1,0:T(8,128)(2,1)}, u32[]{:S(2)}, u32[]{:S(2)}) collective-permute-start(bf16[128,512]{1,0:T(8,128)(2,1)} %get-tuple-element.46), channel_id=1, source_target_pairs={{16,0},{24,8},{17,1},{25,9},{18,2},{26,10},{19,3},{27,11},{20,4},{... | collective-permute-start | bytes 393224 | tf_op jit(solution)/shard_map/ppermute | solution.py:39
  510.8 12.0 %collective-permute-start.9 = (bf16[128,512]{1,0:T(8,128)(2,1)}, bf16[128,512]{1,0:T(8,128)(2,1)}, u32[]{:S(2)}, u32[]{:S(2)}) collective-permute-start(bf16[128,512]{1,0:T(8,128)(2,1)} %get-tuple-element.43), channel_id=1, source_target_pairs={{8,0},{16,8},{24,16},{9,1},{17,9},{25,17},{10,2},{18,10},{26,18},{... | collective-permute-start | bytes 393224 | tf_op jit(solution)/shard_map/ppermute | solution.py:39
  650.5 62.3 %collective-permute-start.15 = (f32[40,1536]{1,0:T(8,128)}, f32[40,1536]{1,0:T(8,128)}, u32[]{:S(2)}, u32[]{:S(2)}) collective-permute-start(f32[40,1536]{1,0:T(8,128)} %fusion), channel_id=1, source_target_pairs={{0,3},{1,4},{2,5},{3,6},{4,7},{5,8},{6,9},{7,10},{8,11},{9,12},{10... | collective-permute-start | bytes 737288
  653.7 59.0 %collective-permute-start.14 = (f32[40,1536]{1,0:T(8,128)}, f32[40,1536]{1,0:T(8,128)}, u32[]{:S(2)}, u32[]{:S(2)}) collective-permute-start(f32[40,1536]{1,0:T(8,128)} %fusion), channel_id=1, source_target_pairs={{0,2},{1,3},{2,4},{3,5},{4,6},{5,7},{6,8},{7,9},{8,10},{9,11},{10,... | collective-permute-start | bytes 737288
  661.0 51.7 %collective-permute-start.13 = (f32[40,1536]{1,0:T(8,128)}, f32[40,1536]{1,0:T(8,128)}, u32[]{:S(2)}, u32[]{:S(2)}) collective-permute-start(f32[40,1536]{1,0:T(8,128)} %fusion), channel_id=1, source_target_pairs={{0,1},{1,2},{2,3},{3,4},{4,5},{5,6},{6,7},{7,8},{8,9},{9,10},{10,1... | collective-permute-start | bytes 737288
  664.0 48.7 %collective-permute-start.16 = (f32[4,1536]{1,0:T(4,128)}, f32[4,1536]{1,0:T(4,128)}, u32[]{:S(2)}, u32[]{:S(2)}) collective-permute-start(f32[4,1536]{1,0:T(4,128)} %slice.146), channel_id=1, source_target_pairs={{0,4},{1,5},{2,6},{3,7},{4,8},{5,9},{6,10},{7,11},{8,12},{9,13},{1... | collective-permute-start | bytes 73736
  (63 other events, 613.0 us)
Sparse Core Ops, SparseCore 0:
  59.0 101.6 all-gather.6
  189.8 28.4 all-gather.8
  220.2 34.9 all-gather.10
  256.9 35.6 all-gather.12
  294.4 35.6 all-gather.14
  336.9 47.6 reduce-scatter.10
  390.7 29.6 all-gather.16
  437.5 46.9 reduce-scatter.12
  488.0 104.7 reduce-scatter.16
  598.7 126.9 reduce-scatter.14
